TPU v7x, 32 devices: a whole 2x2x4 slice. The times are simulated.
32 devices in a mesh: grp: 2 (over x), det: 16 (over z, y, core).
Axes of the slice: x: 2, y: 2, z: 4, core: 2. Of those that a mesh axis runs over, the one named last changes fastest.
Arguments:
- timestream: float32 [2, 1024, 16384], P('grp', 'det'), parts along dimension 0, may hold values from -6 to 6
- gains: float32 [2, 1024], P('grp', 'det'), parts along dimension 0, may hold values from 0.5 to 2
- mode_pattern: float32 [2048, 256], P('grp'), parts along dimension 0, may hold values from -0.375 to 0.375
- mode_weights: float32 [2048, 256], P('grp'), parts along dimension 0, may hold values from -0.1875 to 0.1875
- noise_weight: float32 [2048, 16384], P(('grp', 'det')), parts along dimension 0, may hold values from 0.05 to 1
- block_ids: int32 [2, 1024, 64], P('grp', 'det'), parts along dimension 0, may hold values from 0 to 255
- hits: int32 [2, 1024, 64], P('grp', 'det'), parts along dimension 0, may hold values from 0 to 3
- sky_rows: int32 [512], P('grp'), parts along dimension 0, may hold values from 0 to 255, each once
Outputs:
- filtered: float32 [2, 1024, 16384], P('grp', 'det'), parts along dimension 0
- sky_map: float32 [512, 256], P(('grp', 'det')), parts along dimension 0
There are 2 independent parts, one for each index of `grp`. A program takes and returns all parts, laid end to end along the dimension named above; each array names one. Nothing has to cross between parts.
Inputs may be any that keep to these rules, and one draw needn't show every extreme that they name: `sky_rows`: each row number appears exactly once.
All inputs are finite; a program needn't handle non-finite values.
Results may differ from a plain program's by a relative error of at most 0.000078.
Values sent between devices are 32-bit elements; how exact they have to be, the bound alone decides.
No kernel may reach another device: no remote copies, remote signals or barrier semaphores. Data moves between devices by JAX's collectives and lax.ppermute only.
A program may use at most 128 MiB of HBM per device.

v0:
```python
import math
import jax
import jax.numpy as jnp
from jax import lax
from jax.sharding import PartitionSpec as P

SIDE = 128
PIX = 256


def dft_tables(side):
    first = lax.broadcasted_iota(jnp.int32, (side, side), 0)
    second = lax.broadcasted_iota(jnp.int32, (side, side), 1)
    angle = (first * second % side).astype(jnp.float32) * (2.0 * math.pi / side)
    return (jnp.cos(angle), jnp.sin(angle))


def twiddle_tables(side):
    first = lax.broadcasted_iota(jnp.int32, (side, side), 0)
    second = lax.broadcasted_iota(jnp.int32, (side, side), 1)
    angle = (first * second).astype(jnp.float32) * (2.0 * math.pi / (side * side))
    return (jnp.cos(angle), jnp.sin(angle))


def shards(timestream, gains, mode_pattern, mode_weights, noise_weight, block_ids, hits, sky_rows):
    highest = lax.Precision.HIGHEST
    det_local = timestream.shape[1]
    samples = timestream.shape[2]
    calibrated = timestream / gains[:, :, None]
    slab = lax.all_to_all(calibrated, "det", split_axis=2, concat_axis=1, tiled=True)
    coeff = jnp.einsum("dr,odc->orc", mode_weights, slab, precision=highest)
    corrected = slab - jnp.einsum("dr,orc->odc", mode_pattern, coeff, precision=highest)
    cos_table, sin_table = dft_tables(SIDE)
    twist_cos, twist_sin = twiddle_tables(SIDE)
    spectral_weight = noise_weight.reshape(det_local, SIDE, SIDE)
    slab = lax.all_to_all(corrected, "det", split_axis=1, concat_axis=2, tiled=True)
    items = slab.shape[0]
    signal = slab.reshape(items * det_local, SIDE, SIDE)
    section_real = jnp.einsum("kn,rnm->rkm", cos_table, signal, precision=highest)
    section_imag = -jnp.einsum("kn,rnm->rkm", sin_table, signal, precision=highest)
    turned_real = section_real * twist_cos + section_imag * twist_sin
    turned_imag = section_imag * twist_cos - section_real * twist_sin
    freq_real = jnp.einsum("rkn,nj->rjk", turned_real, cos_table, precision=highest) + jnp.einsum(
        "rkn,nj->rjk", turned_imag, sin_table, precision=highest
    )
    freq_imag = jnp.einsum("rkn,nj->rjk", turned_imag, cos_table, precision=highest) - jnp.einsum(
        "rkn,nj->rjk", turned_real, sin_table, precision=highest
    )
    freq_real = (freq_real.reshape(items, det_local, SIDE, SIDE) * spectral_weight).reshape(
        items * det_local, SIDE, SIDE
    )
    freq_imag = (freq_imag.reshape(items, det_local, SIDE, SIDE) * spectral_weight).reshape(
        items * det_local, SIDE, SIDE
    )
    back_real = jnp.einsum("rjk,jm->rkm", freq_real, cos_table, precision=highest) - jnp.einsum(
        "rjk,jm->rkm", freq_imag, sin_table, precision=highest
    )
    back_imag = jnp.einsum("rjk,jm->rkm", freq_imag, cos_table, precision=highest) + jnp.einsum(
        "rjk,jm->rkm", freq_real, sin_table, precision=highest
    )
    final_real = back_real * twist_cos - back_imag * twist_sin
    final_imag = back_imag * twist_cos + back_real * twist_sin
    result = jnp.einsum("nk,rkm->rnm", cos_table, final_real, precision=highest) - jnp.einsum(
        "nk,rkm->rnm", sin_table, final_imag, precision=highest
    )
    filtered = (result / samples).reshape(items, det_local, samples)
    tile_rows = filtered.reshape(-1, PIX)
    weight = hits.reshape(-1).astype(jnp.float32)
    ids_flat = block_ids.reshape(-1)
    blocks = sky_rows.shape[0]
    ladder = lax.broadcasted_iota(jnp.int32, (blocks, ids_flat.shape[0]), 0)
    rows = jnp.sum(jnp.where(ids_flat[None, :] == ladder, sky_rows[:, None], 0), axis=0)
    table = jnp.where(rows[None, :] == ladder, weight[None, :], 0.0)
    sums = jnp.dot(table, tile_rows, precision=highest, preferred_element_type=jnp.float32)
    counts = jnp.sum(table, axis=1)
    own_sums, own_counts = (
        lax.psum_scatter(sums, "det", scatter_dimension=0, tiled=True),
        lax.psum_scatter(counts, "det", scatter_dimension=0, tiled=True),
    )
    sky_map = own_sums / jnp.sqrt(1.0 + own_counts)[:, None]
    return (filtered, sky_map)


def solution(mesh):
    in_specs = (
        P("grp", "det", None),
        P("grp", "det"),
        P("grp", None),
        P("grp", None),
        P(("grp", "det"), None),
        P("grp", "det", None),
        P("grp", "det", None),
        P("grp"),
    )
    out_specs = (P("grp", "det", None), P(("grp", "det"), None))
    return jax.shard_map(shards, mesh=mesh, in_specs=in_specs, out_specs=out_specs, check_vma=False)
```

profile of v0, /device:TPU:0, one launch (start us, length us, event | category | flops | bytes accessed | tf_op | source)
XLA Modules:
  0.0 547.4 jit_solution(1143022647342395061)
XLA Ops:
  7.2 4.7 broadcast_divide_fusion
  11.9 17.1 %copy.141 = f32[1,64,16384]{1,0,2:T(1,128)} copy(f32[1,64,16384]{2,1,0:T(8,128)} %broadcast_divide_fusion) | data formatting | bytes 8388608 | tf_op jit(solution)/shard_map/div | solution.py:29
  29.0 0.5 broadcast.67
  29.5 74.5 %reduce = f32[16384,64]{1,0:T(8,128)} reduce(f32[16384,1,64]{2,1,0:T(1,128)} %bitcast.98, f32[]{:T(128)} %broadcast.67), dimensions={1}, to_apply=%bitcast.83.reduce_sub_computation | reduce | bytes 8388612
  103.9 13.3 %reshape.70 = f32[16,1,65536]{2,1,0:T(1,128)} reshape(f32[16384,64]{1,0:T(8,128)} %reduce) | data formatting | bytes 8388608
  117.2 100.1 %all_to_all.33 = f32[16,1,65536]{2,1,0:T(1,128)} all-to-all(f32[16,1,65536]{2,1,0:T(1,128)} %reshape.70), channel_id=1, replica_groups=mesh['grp'=2,'det'=16] {'det'}, dimensions={0} | all-to-all | bytes 8388608 | tf_op jit(solution)/shard_map/all_to_all | solution.py:30
  217.3 13.8 %reduce.1 = f32[16,65536]{1,0:T(8,128)} reduce(f32[16,1,65536]{2,1,0:T(1,128)} %all_to_all.33, f32[]{:T(128)} %broadcast.67), dimensions={1}, to_apply=%all_to_all.24.reduce_sub_computation | reduce | bytes 8388612 | tf_op jit(solution)/shard_map/all_to_all | solution.py:30
  231.1 14.0 %reshape.71 = f32[16384,1,64]{2,1,0:T(1,128)} reshape(f32[16,65536]{1,0:T(8,128)} %reduce.1) | data formatting | bytes 8388608
  245.1 7.3 %copy.189 = f32[1,64,16,1024]{3,2,1,0:T(8,128)} copy(f32[1,64,16,1024]{1,3,2,0:T(8,128)} %bitcast.99) | data formatting | bytes 8388608 | tf_op jit(solution)/shard_map/all_to_all | solution.py:30
  252.4 6.5 %copy.143 = f32[1,16,64,1024]{3,2,1,0:T(8,128)} copy(f32[1,16,64,1024]{3,1,2,0:T(8,128)} %bitcast.100) | data formatting | bytes 8388608 | tf_op jit(solution)/shard_map/all_to_all | solution.py:30
  258.9 5.4 copy.145
  264.4 8.8 %convolution_bitcast_fusion = f32[256,1024]{0,1:T(8,128)S(1)} fusion(f32[1024,1024]{1,0:T(8,128)} %bitcast.97, f32[1024,256]{1,0:T(8,128)S(1)} %copy-done.5), kind=kOutput, calls=%fused_computation.34 | convolution fusion | flops 3221225472 | bytes 6291456 | tf_op jit(solution)/shard_map/dr,odc->orc/dot_general | solution.py:31
  273.2 5.2 bitcast_subtract_fusion
  278.4 11.0 %copy.146 = f32[1,1024,1024]{2,0,1:T(1,128)} copy(f32[1,1024,1024]{1,2,0:T(8,128)} %bitcast_subtract_fusion) | data formatting | bytes 8388608 | tf_op jit(solution)/shard_map/sub | solution.py:32
  289.4 5.4 all-to-all-start.1
  294.8 0.2 fusion.47
  295.1 0.1 copy.149
  295.2 0.2 fusion.46
  295.4 0.1 copy.151
  295.5 5.0 copy.194
  300.5 0.1 convert_element_type.62
  300.7 0.7 select_reduce_fusion.1
  301.4 70.9 %all-to-all-done.1 = f32[1,1024,1024]{2,0,1:T(1,128)} async-done(((f32[1,1024,1024]{2,0,1:T(1,128)}), f32[1,1024,1024]{2,0,1:T(1,128)}, u32[]{:S(2)}, u32[]{:S(2)}) %all-to-all-start.1) | async-done | bytes 4194336 | tf_op jit(solution)/shard_map/all_to_all | solution.py:36
  372.3 3.2 copy.193
  375.5 4.4 copy.147
  379.9 4.9 reshape.61
  384.8 9.5 %fusion.35 = f32[64,128,128]{2,1,0:T(8,128)S(1)} fusion(f32[64,128,128]{2,1,0:T(8,128)} %reshape.61), kind=kOutput, calls=%fused_computation.48 | convolution fusion | flops 1610842112 | bytes 8388608 | tf_op jit(solution)/shard_map/kn,rnm->rkm/dot_general | solution.py:40
  394.3 7.0 %fusion.43 = f32[64,128,128]{2,1,0:T(8,128)S(1)} fusion(f32[64,128,128]{2,1,0:T(8,128)S(1)} %copy-done.3), kind=kOutput, calls=%fused_computation.56 | convolution fusion | flops 1610842112 | bytes 8388608 | tf_op jit(solution)/shard_map/kn,rnm->rkm/dot_general | solution.py:39
  401.4 4.7 fusion.21
  406.1 4.8 fusion.25
  410.9 5.1 bitcast_multiply_fusion
  416.0 4.8 fusion.39
  420.8 5.2 bitcast_multiply_fusion.1
  426.0 4.5 fusion.41
  430.5 5.1 convolution_add_fusion
  435.7 4.7 convolution_subtract_fusion
  440.4 4.1 fusion.4
  444.5 5.7 %multiply_bitcast_fusion = f32[64,128,128]{1,2,0:T(8,128)} fusion(f32[64,128,128]{2,1,0:T(8,128)S(1)} %fusion.4, f32[64,128,128]{1,2,0:T(8,128)S(1)} %convolution_add_fusion, f32[64,128,128]{1,2,0:T(8,128)S(1)} %convolution_subtract_fusion, f32[128,128]{0,1:T(8,128)S(1)} %copy.151, f32[128,128]{0,1:T(8,128)S(1)} %copy.149), kind=kOutput, calls=%fused_computation.15 | convolution fusion | flops 1616084992 | bytes 16908288 | tf_op jit(solution)/shard_map/nk,rkm->rnm/dot_general | solution.py:63
  450.2 5.8 %copy.168 = f32[64,128,128]{2,1,0:T(8,128)} copy(f32[64,128,128]{1,2,0:T(8,128)} %multiply_bitcast_fusion) | data formatting | bytes 8388608 | tf_op jit(solution)/shard_map/div | solution.py:66
  455.9 5.2 reshape_reshape.3
  461.1 6.9 %fusion = f32[256,256]{1,0:T(8,128)} fusion(f32[4096,256]{1,0:T(8,128)} %reshape_reshape.3, f32[4096]{0:T(1024)S(1)} %convert_element_type.62, s32[4096]{0:T(1024)S(1)} %select_reduce_fusion.1), kind=kOutput, calls=%fused_computation.1 | convolution fusion | flops 3223322624 | bytes 4489216 | tf_op jit(solution)/shard_map/dot_general | solution.py:74
  468.0 0.6 dynamic-slice
  469.3 0.6 select_reduce_fusion
  469.9 47.8 %all-reduce = f32[256]{0:T(256)S(1)} all-reduce(f32[256]{0:T(256)S(1)} %select_reduce_fusion), channel_id=3, replica_groups=mesh['grp'=2,'det'=16] {'det'}, use_global_device_ids=true, to_apply=%region_3.4.clone | all-reduce | flops 256 | bytes 2048
  517.7 0.1 fusion.65
  517.7 5.0 reshape.62
  522.8 16.2 %reduce-scatter.2.cloned.1.call-done = f32[16,256]{1,0:T(8,128)} async-done(((f32[256,256]{1,0:T(8,128)}), f32[16,256]{1,0:T(8,128)}) %reduce-scatter.2.cloned.1.call-update) | async-done | bytes 16400 | tf_op jit(solution)/shard_map/reduce_scatter | solution.py:77
  538.9 1.4 broadcast_divide_fusion.1
  (24 shorter events, 0.2 us)
Async XLA Ops:
  7.2 266.0 %copy-start = (f32[1024,256]{1,0:T(8,128)S(1)}, f32[1024,256]{1,0:T(8,128)}, u32[]{:S(2)}) copy-start(f32[1024,256]{1,0:T(8,128)} %param.10) | copy-start | bytes 3145732
  258.9 5.4 copy-start.5
  264.4 8.8 %copy-start.4 = (f32[1,1024,1024]{1,2,0:T(8,128)S(1)}, f32[1,1024,1024]{1,2,0:T(8,128)}, u32[]{:S(2)}) copy-start(f32[1,1024,1024]{1,2,0:T(8,128)} %copy.145) | copy-start | bytes 12582916
  289.4 82.9 %all-to-all-start.1 = ((f32[1,1024,1024]{2,0,1:T(1,128)}), f32[1,1024,1024]{2,0,1:T(1,128)}, u32[]{:S(2)}, u32[]{:S(2)}) async-start(f32[1,1024,1024]{2,0,1:T(1,128)} %copy.146), calls=%async_computation.1 | async-start | bytes 8388608 | tf_op jit(solution)/shard_map/all_to_all | solution.py:36
  294.8 244.2 %reduce-scatter.2.cloned.1.call-start = ((), (), s32[]{:S(2)}) async-start(), calls=%async_computation.3 | async-start | bytes 278528 | tf_op jit(solution)/shard_map/reduce_scatter | solution.py:77
  295.5 5.0 copy-start.7
  295.5 5.1 copy-start.6
  295.5 5.1 copy-start.8
  384.8 9.5 %copy-start.3 = (f32[64,128,128]{2,1,0:T(8,128)S(1)}, f32[64,128,128]{2,1,0:T(8,128)}, u32[]{:S(2)}) copy-start(f32[64,128,128]{2,1,0:T(8,128)} %reshape.61) | copy-start | bytes 12582916
  406.1 4.8 copy-start.2
  461.1 6.9 %copy-start.9 = (u32[32]{0:T(128)S(1)}, u32[32]{0:T(128)}, u32[]{:S(2)}) copy-start(u32[32]{0:T(128)} %constant.33) | copy-start | bytes 388
  517.7 22.7 %copy-start.1 = (f32[1024,256]{1,0:T(8,128)S(1)}, f32[1024,256]{1,0:T(8,128)}, u32[]{:S(2)}) copy-start(f32[1024,256]{1,0:T(8,128)} %param.10) | copy-start | bytes 3145732
Sparse Core Ops, SparseCore 0:
  468.1 70.7 reduce-scatter.1
where the time goes:
time: 553 us; the launch traced here: 547 us
  blocking collectives  148 us (27%)
  local copies, waits for them, and re-layouts  109 us (20%)
  other arithmetic  96.2 us (17%)
  waiting for transfers between devices  87.1 us (16%)
  matrix products  86.2 us (16%)
  between operations  15.1 us (3%)
    all_to_all x1, blocking collectives, shards(): lax.all_to_all(calibrated, 'det', split_axis=2, concat_axis=1, tiled=True)  100 us
    unnamed x1, other arithmetic  74.5 us
    all_to_all x1, waiting for transfers between devices, shards(): lax.all_to_all(corrected, 'det', split_axis=1, concat_axis=2, tiled=True)  70.9 us
    unnamed x1, blocking collectives  47.8 us
    unnamed x26, local copies, waits for them, and re-layouts  36.5 us
    all_to_all x3, local copies, waits for them, and re-layouts, shards(): lax.all_to_all(calibrated, 'det', split_axis=2, concat_axis=1, tiled=True)  19.3 us
    div x1, local copies, waits for them, and re-layouts, shards(): calibrated = timestream / gains[:, :, None]  17.1 us
    reduce_scatter x1, waiting for transfers between devices, shards(): lax.psum_scatter(sums, 'det', scatter_dimension=0, tiled=True)  16.2 us
  transfers between devices with their start and end apart: 2, of which 2 were waited for; matrix products, arithmetic and copies ran while one was open for 2% of the time, Pallas kernels for 0%

commit v1 on v0

--- a/solution.py
+++ b/solution.py
@@ -27,7 +27,9 @@
     det_local = timestream.shape[1]
     samples = timestream.shape[2]
     calibrated = timestream / gains[:, :, None]
-    slab = lax.all_to_all(calibrated, "det", split_axis=2, concat_axis=1, tiled=True)
+    parts = jnp.split(calibrated, lax.axis_size("det"), axis=2)
+    received = lax.all_to_all(jnp.stack(parts), "det", 0, 0)
+    slab = jnp.concatenate(received, axis=1)
     coeff = jnp.einsum("dr,odc->orc", mode_weights, slab, precision=highest)
     corrected = slab - jnp.einsum("dr,orc->odc", mode_pattern, coeff, precision=highest)
     cos_table, sin_table = dft_tables(SIDE)

time: 553 us -> 404 us (0.73)
  other arithmetic: 96.2 us -> 5.93 us
  local copies, waits for them, and re-layouts: 109 us -> 51.1 us
    unnamed x1 -> x0, other arithmetic: 74.5 us -> none
    unnamed x26 -> x38, local copies, waits for them, and re-layouts: 36.5 us -> 9.09 us
    all_to_all x3 -> x0, local copies, waits for them, and re-layouts: 19.3 us -> none  [shards(): lax.all_to_all(calibrated, 'det', split_axis=2, concat_axis=1, tiled=True)]
    div x1 -> x0, local copies, waits for them, and re-layouts: 17.1 us -> none  [shards(): calibrated = timestream / gains[:, :, None]]
    all_to_all x1 -> x0, other arithmetic: 13.8 us -> none  [shards(): lax.all_to_all(calibrated, 'det', split_axis=2, concat_axis=1, tiled=True)]
  transfers between devices with their start and end apart: 2 -> 2, of which waited for: 2 -> 2; matrix products, arithmetic and copies ran while one was open for 2% -> 3% of each run, Pallas kernels for 0% -> 0%
where the time goes in v1:
time: 404 us; the launch traced here: 398 us
  blocking collectives  147 us (36%)
  waiting for transfers between devices  86.8 us (21%)
  matrix products  85.8 us (21%)
  local copies, waits for them, and re-layouts  51.1 us (13%)
  between operations  15.2 us (4%)
  other arithmetic  5.93 us (1%)
  starting transfers between devices  5.72 us (1%)
    all_to_all x1, blocking collectives, shards(): received = lax.all_to_all(jnp.stack(parts), 'det', 0, 0)  99.4 us
    all_to_all x1, waiting for transfers between devices, shards(): lax.all_to_all(corrected, 'det', split_axis=1, concat_axis=2, tiled=True)  70.6 us
    unnamed x1, blocking collectives  47.8 us
    reduce_scatter x1, waiting for transfers between devices, shards(): lax.psum_scatter(sums, 'det', scatter_dimension=0, tiled=True)  16.2 us
    sub x1, local copies, waits for them, and re-layouts, shards(): slab - jnp.einsum('dr,orc->odc', mode_pattern, coeff, precision=highest)  11 us
    dot_general x1, matrix products, shards(): jnp.einsum('kn,rnm->rkm', sin_table, signal, precision=highest)  9.58 us
    unnamed x38, local copies, waits for them, and re-layouts  9.09 us
    dot_general x1, matrix products, shards(): coeff = jnp.einsum('dr,odc->orc', mode_weights, slab, precision=highest)  8.62 us
  transfers between devices with their start and end apart: 2, of which 2 were waited for; matrix products, arithmetic and copies ran while one was open for 3% of the time, Pallas kernels for 0%

profile of v1, /device:TPU:0, one launch (start us, length us, event | category | flops | bytes accessed | tf_op | source)
XLA Modules:
  0.0 397.8 jit_solution(12811017404580902622)
XLA Ops:
  7.2 0.0 copy-start
  7.2 2.6 broadcast_divide_fusion
  10.3 99.4 %all_to_all.20 = f32[16,1,64,1024]{3,2,1,0:T(8,128)} all-to-all(f32[16,1,64,1024]{3,2,1,0:T(8,128)S(1)} %fusion.27), channel_id=1, replica_groups=mesh['grp'=2,'det'=16] {'det'}, dimensions={0} | all-to-all | bytes 8388608 | tf_op jit(solution)/shard_map/all_to_all | solution.py:31
  109.7 5.4 %copy.94 = f32[1,1024,1024]{1,2,0:T(8,128)} copy(f32[1,1024,1024]{2,1,0:T(8,128)} %bitcast.156) | data formatting | bytes 8388608 | tf_op jit(solution)/shard_map/reshape | solution.py:32
  115.1 8.6 %convolution_bitcast_fusion = f32[256,1024]{0,1:T(8,128)S(1)} fusion(f32[1024,1024]{1,0:T(8,128)} %bitcast.157, f32[1024,256]{1,0:T(8,128)S(1)} %copy-done.5), kind=kOutput, calls=%fused_computation.34 | convolution fusion | flops 3221225472 | bytes 6291456 | tf_op jit(solution)/shard_map/dr,odc->orc/dot_general | solution.py:33
  123.8 5.2 %bitcast_subtract_fusion = f32[1,1024,1024]{1,2,0:T(8,128)} fusion(f32[1,1024,1024]{1,2,0:T(8,128)S(1)} %copy-done.4, f32[256,1024]{0,1:T(8,128)S(1)} %convolution_bitcast_fusion, f32[1024,256]{1,0:T(8,128)S(1)} %copy-done), kind=kOutput, calls=%fused_computation.5 | convolution fusion | flops 3222274048 | bytes 10485760 | tf_op jit(solution)/shard_map/dr,orc->odc/dot_general | solution.py:34
  129.0 11.0 %copy.95 = f32[1,1024,1024]{2,0,1:T(1,128)} copy(f32[1,1024,1024]{1,2,0:T(8,128)} %bitcast_subtract_fusion) | data formatting | bytes 8388608 | tf_op jit(solution)/shard_map/sub | solution.py:34
  140.0 5.4 %all-to-all-start.1 = ((f32[1,1024,1024]{2,0,1:T(1,128)}), f32[1,1024,1024]{2,0,1:T(1,128)}, u32[]{:S(2)}, u32[]{:S(2)}) async-start(f32[1,1024,1024]{2,0,1:T(1,128)} %copy.95), calls=%async_computation.1 | async-start | bytes 8388608 | tf_op jit(solution)/shard_map/all_to_all | solution.py:38
  145.4 0.3 reduce-scatter.2.cloned.1.call-start
  145.7 0.2 fusion.62
  145.9 0.1 copy.100
  146.0 0.2 fusion.63
  146.3 0.1 copy.98
  146.4 0.0 copy-start.7
  146.4 0.0 copy-start.6
  146.4 0.0 copy-start.8
  146.4 5.0 %copy.142 = f32[8,8,128,128]{3,2,1,0:T(8,128)} copy(f32[8,8,128,128]{3,1,2,0:T(8,128)} %bitcast.159) | data formatting | bytes 8388608
  151.4 0.1 convert_element_type.62
  151.5 0.1 eq.20
  151.5 0.7 select_reduce_fusion.1
  152.3 70.6 %all-to-all-done.1 = f32[1,1024,1024]{2,0,1:T(1,128)} async-done(((f32[1,1024,1024]{2,0,1:T(1,128)}), f32[1,1024,1024]{2,0,1:T(1,128)}, u32[]{:S(2)}, u32[]{:S(2)}) %all-to-all-start.1) | async-done | bytes 4194336 | tf_op jit(solution)/shard_map/all_to_all | solution.py:38
  222.9 3.2 copy.141
  226.1 4.4 %copy.96 = f32[1,64,16,1024]{3,2,1,0:T(8,128)} copy(f32[1,64,16,1024]{3,1,2,0:T(8,128)S(1)} %bitcast.158) | data formatting | bytes 8388608 | tf_op jit(solution)/shard_map/all_to_all | solution.py:38
  230.5 4.9 %reshape.65 = f32[64,128,128]{2,1,0:T(8,128)} reshape(f32[1,64,16,1024]{3,2,1,0:T(8,128)} %copy.96) | data formatting | bytes 8388608 | tf_op jit(solution)/shard_map/reshape | solution.py:40
  235.4 9.6 %fusion.51 = f32[64,128,128]{2,1,0:T(8,128)S(1)} fusion(f32[64,128,128]{2,1,0:T(8,128)} %reshape.65), kind=kOutput, calls=%fused_computation.80 | convolution fusion | flops 1610842112 | bytes 8388608 | tf_op jit(solution)/shard_map/kn,rnm->rkm/dot_general | solution.py:42
  245.0 7.0 %fusion.59 = f32[64,128,128]{2,1,0:T(8,128)S(1)} fusion(f32[64,128,128]{2,1,0:T(8,128)S(1)} %copy-done.3), kind=kOutput, calls=%fused_computation.88 | convolution fusion | flops 1610842112 | bytes 8388608 | tf_op jit(solution)/shard_map/kn,rnm->rkm/dot_general | solution.py:41
  252.0 4.7 %fusion.21 = f32[128,64,128]{2,0,1:T(8,128)S(1)} fusion(f32[64,128,128]{2,1,0:T(8,128)S(1)} %fusion.59, f32[64,128,128]{2,1,0:T(8,128)S(1)} %fusion.51, f32[128,128]{0,1:T(8,128)S(1)} %copy.100, f32[128,128]{0,1:T(8,128)S(1)} %copy.98), kind=kOutput, calls=%fused_computation.35 | convolution fusion | flops 1615036416 | bytes 12713984 | tf_op jit(solution)/shard_map/rkn,nj->rjk/dot_general | solution.py:48
  256.7 0.0 copy-start.2
  256.7 4.8 %fusion.25 = f32[128,64,128]{2,0,1:T(8,128)S(1)} fusion(f32[64,128,128]{2,1,0:T(8,128)S(1)} %fusion.59, f32[64,128,128]{2,1,0:T(8,128)S(1)} %fusion.51, f32[128,128]{0,1:T(8,128)S(1)} %copy.100, f32[128,128]{0,1:T(8,128)S(1)} %copy.98), kind=kOutput, calls=%fused_computation.36 | convolution fusion | flops 1615036416 | bytes 12713984 | tf_op jit(solution)/shard_map/rkn,nj->rjk/dot_general | solution.py:45
  261.5 5.1 %bitcast_multiply_fusion = f32[64,128,128]{2,1,0:T(8,128)S(1)} fusion(f32[8,8,128,128]{3,2,1,0:T(8,128)S(1)} %copy-done.2, f32[128,64,128]{2,0,1:T(8,128)S(1)} %fusion.21, f32[64,128,128]{2,1,0:T(8,128)S(1)} %fusion.59, f32[64,128,128]{2,1,0:T(8,128)S(1)} %fusion.51, f32[128,128]{0,1:T(8,128)S(1)} %copy.100, f32[128,128]{0,1:T(8,128)S(1)} %copy.98), kind=kOutput, calls=%fused_computation.3 | convolution fusion | flops 1617133568 | bytes 21102592 | tf_op jit(solution)/shard_map/rkn,nj->rjk/dot_general | solution.py:48
  266.6 4.8 %fusion.55 = f32[64,128,128]{1,2,0:T(8,128)S(1)} fusion(f32[64,128,128]{2,1,0:T(8,128)S(1)} %bitcast_multiply_fusion), kind=kOutput, calls=%fused_computation.84 | convolution fusion | flops 1610842112 | bytes 8388608 | tf_op jit(solution)/shard_map/rjk,jm->rkm/dot_general | solution.py:60
  271.4 5.2 %bitcast_multiply_fusion.1 = f32[64,128,128]{2,1,0:T(8,128)S(1)} fusion(f32[8,8,128,128]{3,2,1,0:T(8,128)S(1)} %copy-done.2, f32[128,64,128]{2,0,1:T(8,128)S(1)} %fusion.25, f32[64,128,128]{2,1,0:T(8,128)S(1)} %fusion.59, f32[64,128,128]{2,1,0:T(8,128)S(1)} %fusion.51, f32[128,128]{0,1:T(8,128)S(1)} %copy.100, f32[128,128]{0,1:T(8,128)S(1)} %copy.98), kind=kOutput, calls=%fused_computation.4 | convolution fusion | flops 1617133568 | bytes 21102592 | tf_op jit(solution)/shard_map/rkn,nj->rjk/dot_general | solution.py:45
  276.6 4.5 %fusion.57 = f32[64,128,128]{1,2,0:T(8,128)S(1)} fusion(f32[64,128,128]{2,1,0:T(8,128)S(1)} %bitcast_multiply_fusion.1), kind=kOutput, calls=%fused_computation.86 | convolution fusion | flops 1610842112 | bytes 8388608 | tf_op jit(solution)/shard_map/rjk,jm->rkm/dot_general | solution.py:57
  281.1 5.1 %convolution_add_fusion = f32[64,128,128]{1,2,0:T(8,128)S(1)} fusion(f32[64,128,128]{1,2,0:T(8,128)S(1)} %fusion.55, f32[64,128,128]{2,1,0:T(8,128)S(1)} %bitcast_multiply_fusion.1), kind=kOutput, calls=%fused_computation.24 | convolution fusion | flops 1611890688 | bytes 12582912 | tf_op jit(solution)/shard_map/rjk,jm->rkm/dot_general | solution.py:60
  286.3 4.5 %convolution_subtract_fusion = f32[64,128,128]{1,2,0:T(8,128)S(1)} fusion(f32[64,128,128]{1,2,0:T(8,128)S(1)} %fusion.57, f32[64,128,128]{2,1,0:T(8,128)S(1)} %bitcast_multiply_fusion), kind=kOutput, calls=%fused_computation.25 | convolution fusion | flops 1611890688 | bytes 12582912 | tf_op jit(solution)/shard_map/rjk,jm->rkm/dot_general | solution.py:57
  290.8 4.1 %fusion.4 = f32[64,128,128]{2,1,0:T(8,128)S(1)} fusion(f32[64,128,128]{1,2,0:T(8,128)S(1)} %convolution_subtract_fusion, f32[64,128,128]{1,2,0:T(8,128)S(1)} %convolution_add_fusion, f32[128,128]{0,1:T(8,128)S(1)} %copy.100, f32[128,128]{0,1:T(8,128)S(1)} %copy.98), kind=kOutput, calls=%fused_computation.16 | convolution fusion | flops 1613987840 | bytes 12713984 | tf_op jit(solution)/shard_map/nk,rkm->rnm/dot_general | solution.py:65
  294.9 5.7 %multiply_bitcast_fusion = f32[64,128,128]{1,2,0:T(8,128)} fusion(f32[64,128,128]{2,1,0:T(8,128)S(1)} %fusion.4, f32[64,128,128]{1,2,0:T(8,128)S(1)} %convolution_add_fusion, f32[64,128,128]{1,2,0:T(8,128)S(1)} %convolution_subtract_fusion, f32[128,128]{0,1:T(8,128)S(1)} %copy.100, f32[128,128]{0,1:T(8,128)S(1)} %copy.98), kind=kOutput, calls=%fused_computation.15 | convolution fusion | flops 1616084992 | bytes 16908288 | tf_op jit(solution)/shard_map/nk,rkm->rnm/dot_general | solution.py:65
  300.6 5.8 %copy.117 = f32[64,128,128]{2,1,0:T(8,128)} copy(f32[64,128,128]{1,2,0:T(8,128)} %multiply_bitcast_fusion) | data formatting | bytes 8388608 | tf_op jit(solution)/shard_map/div | solution.py:68
  306.3 5.2 %reshape_reshape.3 = f32[4096,256]{1,0:T(8,128)} reshape(f32[64,128,128]{2,1,0:T(8,128)} %copy.117) | data formatting | bytes 8388608 | tf_op jit(solution)/shard_map/reshape;reshape | solution.py:69
  311.5 6.9 %fusion = f32[256,256]{1,0:T(8,128)} fusion(f32[4096,256]{1,0:T(8,128)} %reshape_reshape.3, f32[4096]{0:T(1024)S(1)} %convert_element_type.62, s32[4096]{0:T(1024)S(1)} %select_reduce_fusion.1), kind=kOutput, calls=%fused_computation.1 | convolution fusion | flops 3223322624 | bytes 4489216 | tf_op jit(solution)/shard_map/dot_general | solution.py:76
  318.4 0.0 reduce-scatter.2.cloned.1.call-update
  318.4 0.6 dynamic-slice
  319.7 0.6 select_reduce_fusion
  320.3 47.8 %all-reduce = f32[256]{0:T(256)S(1)} all-reduce(f32[256]{0:T(256)S(1)} %select_reduce_fusion), channel_id=3, replica_groups=mesh['grp'=2,'det'=16] {'det'}, use_global_device_ids=true, to_apply=%region_3.4.clone | all-reduce | flops 256 | bytes 2048
  368.1 0.1 fusion.81
  368.1 5.0 %reshape.66 = f32[1,64,16384]{2,1,0:T(8,128)} reshape(f32[64,128,128]{2,1,0:T(8,128)} %copy.117) | data formatting | bytes 8388608 | tf_op jit(solution)/shard_map/reshape | solution.py:68
  373.2 16.2 %reduce-scatter.2.cloned.1.call-done = f32[16,256]{1,0:T(8,128)} async-done(((f32[256,256]{1,0:T(8,128)}), f32[16,256]{1,0:T(8,128)}) %reduce-scatter.2.cloned.1.call-update) | async-done | bytes 16400 | tf_op jit(solution)/shard_map/reduce_scatter | solution.py:79
  389.3 1.4 broadcast_divide_fusion.1
  (32 shorter events, 0.4 us)
Async XLA Ops:
  7.2 116.6 %copy-start = (f32[1024,256]{1,0:T(8,128)S(1)}, f32[1024,256]{1,0:T(8,128)}, u32[]{:S(2)}) copy-start(f32[1024,256]{1,0:T(8,128)} %param.10) | copy-start | bytes 3145732
  109.7 5.4 %copy-start.5 = (f32[1024,256]{1,0:T(8,128)S(1)}, f32[1024,256]{1,0:T(8,128)}, u32[]{:S(2)}) copy-start(f32[1024,256]{1,0:T(8,128)} %param.11) | copy-start | bytes 3145732
  115.1 8.6 %copy-start.4 = (f32[1,1024,1024]{1,2,0:T(8,128)S(1)}, f32[1,1024,1024]{1,2,0:T(8,128)}, u32[]{:S(2)}) copy-start(f32[1,1024,1024]{1,2,0:T(8,128)} %copy.94) | copy-start | bytes 12582916
  140.0 82.9 %all-to-all-start.1 = ((f32[1,1024,1024]{2,0,1:T(1,128)}), f32[1,1024,1024]{2,0,1:T(1,128)}, u32[]{:S(2)}, u32[]{:S(2)}) async-start(f32[1,1024,1024]{2,0,1:T(1,128)} %copy.95), calls=%async_computation.1 | async-start | bytes 8388608 | tf_op jit(solution)/shard_map/all_to_all | solution.py:38
  145.4 244.0 %reduce-scatter.2.cloned.1.call-start = ((), (), s32[]{:S(2)}) async-start(), calls=%async_computation.3 | async-start | bytes 278528 | tf_op jit(solution)/shard_map/reduce_scatter | solution.py:79
  146.4 5.0 %copy-start.7 = (s32[1,64,64]{2,1,0:T(8,128)S(1)}, s32[1,64,64]{2,1,0:T(8,128)}, u32[]{:S(2)}) copy-start(s32[1,64,64]{2,1,0:T(8,128)} %param.14) | copy-start | bytes 49156
  146.4 5.1 %copy-start.6 = (s32[1,64,64]{2,1,0:T(8,128)S(1)}, s32[1,64,64]{2,1,0:T(8,128)}, u32[]{:S(2)}) copy-start(s32[1,64,64]{2,1,0:T(8,128)} %param.13) | copy-start | bytes 49156
  146.4 5.1 %copy-start.8 = (s32[256]{0:T(256)S(1)}, s32[256]{0:T(256)}, u32[]{:S(2)}) copy-start(s32[256]{0:T(256)} %param.15) | copy-start | bytes 3076
  235.4 9.6 %copy-start.3 = (f32[64,128,128]{2,1,0:T(8,128)S(1)}, f32[64,128,128]{2,1,0:T(8,128)}, u32[]{:S(2)}) copy-start(f32[64,128,128]{2,1,0:T(8,128)} %reshape.65) | copy-start | bytes 12582916
  256.7 4.8 %copy-start.2 = (f32[8,8,128,128]{3,2,1,0:T(8,128)S(1)}, f32[8,8,128,128]{3,2,1,0:T(8,128)}, u32[]{:S(2)}) copy-start(f32[8,8,128,128]{3,2,1,0:T(8,128)} %copy.142) | copy-start | bytes 12582916
  311.5 6.9 %copy-start.9 = (u32[32]{0:T(128)S(1)}, u32[32]{0:T(128)}, u32[]{:S(2)}) copy-start(u32[32]{0:T(128)} %constant.33) | copy-start | bytes 388
  368.1 22.7 %copy-start.1 = (f32[1024,256]{1,0:T(8,128)S(1)}, f32[1024,256]{1,0:T(8,128)}, u32[]{:S(2)}) copy-start(f32[1024,256]{1,0:T(8,128)} %param.10) | copy-start | bytes 3145732
Sparse Core Ops, SparseCore 0:
  318.6 70.7 reduce-scatter.1
